TPU v7x, 256 devices: a whole 4x4x8 slice. The times are simulated.
256 devices in a mesh: mem: 16 (over x_hi, y, core), tile: 16 (over x_lo, z).
Axes of the slice: x: 4 (x_hi: 2, x_lo: 2; x = x_hi * 2 + x_lo), y: 4, z: 8, core: 2. Of those that a mesh axis runs over, the one named last changes fastest.
Arguments:
- alpha: bfloat16 [16, 16, 720, 1440], P('mem', None, 'tile'), may hold values from -6 to 6
- perturbation: bfloat16 [16, 16, 720, 1440], P('mem', None, 'tile'), may hold values from -3 to 3
- lon_scale: float32 [16], replicated, may hold values from 8 to 48
- lat_scale: float32 [16], replicated, may hold values from 12 to 64
- obs_level: int32 [16, 16384], P('tile'), may hold values from 0 to 15
- obs_row: int32 [16, 16384], P('tile'), may hold values from 0 to 44
- obs_col: int32 [16, 16384], P('tile'), may hold values from 0 to 1439
- obs_count: int32 [16], P('tile'), may hold values from 8192 to 16384, as said below
- innovation: float32 [16, 16384], P('tile'), may hold values from -12 to 12
- obs_weight: float32 [16, 16384], P('tile'), may hold values from 1 to 8
Outputs:
- gradient: bfloat16 [16, 16, 720, 1440], P('mem', None, 'tile')
Inputs may be any that keep to these rules, and one draw needn't show every extreme that they name: Observations of band t fill slots 0 to obs_count[t] - 1; the other slots carry no observation. Some band is full in every draw.
All inputs are finite; a program needn't handle non-finite values.
Results may differ from a plain program's by a relative error of at most 0.0056.
Values may be sent and summed in bfloat16 or wider, within the bound.
No kernel may reach another device: no remote copies, remote signals or barrier semaphores. Data moves between devices by JAX's collectives and lax.ppermute only.
A program may use at most 128 MiB of HBM per device.

v0:
```python
import jax
import jax.numpy as jnp
from jax import lax
from jax.sharding import PartitionSpec as P


def square_root(lengths, extent, periodic):
    positions = jnp.arange(extent).astype(jnp.float32)
    distance = jnp.abs(positions[:, None] - positions[None, :])
    if periodic:
        distance = jnp.minimum(distance, extent - distance)
    scales = lengths[:, None, None]
    factor = (2.0 / jnp.pi) ** 0.25
    values = factor * jnp.exp(-((distance[None] / scales) ** 2)) / jnp.sqrt(scales)
    return values.astype(jnp.bfloat16)


def localize(values_in, lat_root, lon_root):
    zonal = jnp.einsum(
        "klab,lbc->klac", values_in, lon_root, preferred_element_type=jnp.float32
    ).astype(jnp.bfloat16)
    return jnp.einsum("lab,klbc->klac", lat_root, zonal, preferred_element_type=jnp.float32)


def pick_cells(flat_rows, row_place, column):
    slots = row_place.shape[0]
    block = min(4096, slots)
    width = flat_rows.shape[1]
    counter = jnp.arange(width)

    def pick_one_block(pair):
        rows_here, cols_here = pair
        taken = flat_rows[rows_here]
        return jnp.sum(jnp.where(counter[None, :] == cols_here[:, None], taken, 0.0), axis=1)

    picked = lax.map(pick_one_block, (row_place.reshape(-1, block), column.reshape(-1, block)))
    return picked.reshape(-1)


def place_cells(row_total, width, row_place, column, values):
    slots = row_place.shape[0]
    block = min(4096, slots)
    counter = jnp.arange(width)

    def place_one_block(field, triple):
        rows_here, cols_here, vals_here = triple
        lines = jnp.where(counter[None, :] == cols_here[:, None], vals_here[:, None], 0.0)
        return (field.at[rows_here].add(lines, mode="drop"), jnp.float32(0.0))

    start_field = jnp.zeros((row_total, width), jnp.float32)
    triples = (row_place.reshape(-1, block), column.reshape(-1, block), values.reshape(-1, block))
    return lax.scan(place_one_block, start_field, triples)[0]


def shards(
    alpha,
    perturbation,
    lon_scale,
    lat_scale,
    obs_level,
    obs_row,
    obs_col,
    obs_count,
    innovation,
    obs_weight,
):
    level_count = alpha.shape[1]
    row_count = alpha.shape[2]
    column_count = alpha.shape[3]
    tile_count = lax.axis_size("tile")
    tile_index = lax.axis_index("tile")
    slab_levels = level_count // tile_count
    first_level = tile_index * slab_levels
    lon_part = lax.dynamic_slice_in_dim(lon_scale, first_level, slab_levels)
    lat_part = lax.dynamic_slice_in_dim(lat_scale, first_level, slab_levels)
    lon_root = square_root(lon_part, column_count, True)
    lat_root = square_root(lat_part, row_count * tile_count, False)
    level_index = obs_level[0]
    row_index = obs_row[0]
    column = obs_col[0]
    slot_count = obs_level.shape[1]
    valid = jnp.arange(slot_count) < obs_count[0]
    band_line = level_index * row_count + row_index
    alpha_slab = lax.all_to_all(alpha, "tile", split_axis=1, concat_axis=2, tiled=True)
    spread_slab = localize(alpha_slab, lat_root, lon_root).astype(jnp.bfloat16)
    spread_band = lax.all_to_all(spread_slab, "tile", split_axis=2, concat_axis=1, tiled=True)
    partial_field = jnp.sum(
        perturbation.astype(jnp.float32) * spread_band.astype(jnp.float32), axis=0
    )
    total_field = lax.psum(partial_field, "mem")
    model_obs = pick_cells(total_field.reshape(-1, column_count), band_line, column)
    weighted = jnp.where(valid, obs_weight[0] * (model_obs - innovation[0]), 0.0)
    obs_field = place_cells(level_count * row_count, column_count, band_line, column, weighted)
    obs_field = obs_field.reshape(level_count, row_count, column_count)
    sensitive = (perturbation.astype(jnp.float32) * obs_field[None]).astype(jnp.bfloat16)
    sensitive_slab = lax.all_to_all(sensitive, "tile", split_axis=1, concat_axis=2, tiled=True)
    gradient_slab = (
        alpha_slab.astype(jnp.float32) + localize(sensitive_slab, lat_root, lon_root)
    ).astype(jnp.bfloat16)
    return lax.all_to_all(gradient_slab, "tile", split_axis=2, concat_axis=1, tiled=True)


def solution(mesh):
    in_specs = (
        P("mem", None, "tile", None),
        P("mem", None, "tile", None),
        P(),
        P(),
        P("tile", None),
        P("tile", None),
        P("tile", None),
        P("tile"),
        P("tile", None),
        P("tile", None),
    )
    out_specs = P("mem", None, "tile", None)
    return jax.shard_map(shards, mesh=mesh, in_specs=in_specs, out_specs=out_specs, check_vma=False)
```

profile of v0, /device:TPU:34, one launch (start us, length us, event | category | flops | bytes accessed | tf_op | source)
XLA Modules:
  0.0 922.1 jit_solution(17614433650385890455)
XLA Ops:
  6.5 4.3 copy.32
  10.8 9.5 %all-to-all-start = ((bf16[1,16,45,1440]{3,2,0,1:T(8,128)(2,1)}), bf16[1,16,45,1440]{3,2,0,1:T(8,128)(2,1)S(1)}, u32[]{:S(2)}, u32[]{:S(2)}) async-start(bf16[1,16,45,1440]{3,2,0,1:T(8,128)(2,1)} %copy.32), calls=%async_computation | async-start | bytes 4718592 | tf_op jit(solution)/shard_map/all_to_all | solution.py:84
  20.3 0.0 all-reduce.2.cloned.1.call-start
  20.4 0.6 dynamic_slice.23
  21.7 0.7 dynamic_slice.24
  23.2 50.1 %all-to-all-done = bf16[1,16,45,1440]{3,2,0,1:T(8,128)(2,1)S(1)} async-done(((bf16[1,16,45,1440]{3,2,0,1:T(8,128)(2,1)}), bf16[1,16,45,1440]{3,2,0,1:T(8,128)(2,1)S(1)}, u32[]{:S(2)}, u32[]{:S(2)}) %all-to-all-start) | async-done | bytes 2073632 | tf_op jit(solution)/shard_map/all_to_all | solution.py:84
  73.3 2.1 reshape.399
  75.5 11.9 %fusion.29 = bf16[1,1,720,1440]{2,3,0,1:T(8,128)(2,1)} fusion(bf16[720,1440]{1,0:T(8,128)(2,1)} %reshape.399, f32[]{:T(128)} %bitcast.1, f32[]{:T(128)} %bitcast, f32[1440]{0:T(1024)S(1)} %iota_convert_fusion, f32[]{:T(128)} %bitcast.8, f32[]{:T(128)} %bitcast.7, f32[720]{0:T(1024)S(1)} %iota_convert_fusion.1), kind=kOutput, calls=%fused_computation.37 | convolution fusion | flops 4505932800 | bytes 4155856 | tf_op jit(solution)/shard_map/lab,klbc->klac/dot_general | solution.py:22
  87.3 12.1 %copy.33 = bf16[1,1,720,1440]{3,0,1,2:T(2,128)(2,1)} copy(bf16[1,1,720,1440]{2,3,0,1:T(8,128)(2,1)} %fusion.29) | data formatting | bytes 4147200 | tf_op jit(solution)/shard_map/convert_element_type | solution.py:85
  99.4 0.5 broadcast.349
  99.9 13.8 %reduce.18 = bf16[720,1440]{1,0:T(8,128)(2,1)S(1)} reduce(bf16[720,1,1,1440]{3,2,1,0:T(2,128)(2,1)} %bitcast.101, bf16[]{:T(256)} %broadcast.349), dimensions={1,2}, to_apply=%bitcast.69.reduce_sub_computation | reduce | bytes 4147202
  113.8 5.3 reshape.462
  119.0 56.9 %all_to_all.19 = bf16[16,2,32400]{2,1,0:T(2,128)(2,1)S(1)} all-to-all(bf16[16,2,32400]{2,1,0:T(2,128)(2,1)} %reshape.462), channel_id=1, replica_groups=mesh['mem'=16,'tile'=16] {'tile'}, dimensions={0} | all-to-all | bytes 4147200 | tf_op jit(solution)/shard_map/all_to_all | solution.py:86
  176.0 8.7 reshape.463
  184.7 9.0 convert.2
  193.7 3.1 convert_multiply_fusion.1
  196.9 4.7 copy.35
  201.6 4.1 reshape.401
  205.7 0.5 broadcast.346
  206.2 0.3 copy-done.8
  206.5 0.8 reduce.14
  207.4 0.2 add_reduce_fusion
  207.6 0.6 broadcast.347
  208.2 0.8 reduce.15
  209.0 0.7 squeeze.23
  209.7 0.8 reduce.16
  210.5 0.6 squeeze.24
  211.8 147.9 %all-reduce.2.cloned.1.call-done = f32[720,1440]{1,0:T(8,128)} async-done(((f32[720,1440]{1,0:T(8,128)}), f32[720,1440]{1,0:T(8,128)}) %all-reduce.2.cloned.1.call-update) | async-done | bytes 4147216 | tf_op jit(solution)/shard_map/psum | solution.py:90
  359.7 162.5 %while.24 = (s32[]{:T(128)}, f32[4,4096]{1,0:T(4,128)S(1)}, s32[4,4096]{1,0:T(4,128)S(1)}, s32[4,4096]{1,0:T(4,128)S(1)}, f32[720,1440]{1,0:T(8,128)}) while((s32[]{:T(128)}, f32[4,4096]{1,0:T(4,128)S(1)}, s32[4,4096]{1,0:T(4,128)S(1)}, s32[4,4096]{1,0:T(4,128)S(1)}, f32[720,1440]{1,0:T(8,128)}) %tuple.43), condition=%wide.region_3.4_spmd.clone.clone, body=%wide.region_1.3_spmd.clone.sunk.clone | while | flops 17707008 | bytes 70959168 | solution.py:36
  359.8 29.5 %gather_fusion = f32[4096,1440]{1,0:T(8,128)} fusion(f32[720,1440]{1,0:T(8,128)} %get-tuple-element.217, s32[4096]{0:T(1024)S(1)} %broadcast_clamp_fusion.3), kind=kCustom, calls=%fused_computation.clone.clone.1.clone | custom fusion | bytes 47202304 | tf_op jit(solution)/shard_map/while/body/eval_jaxpr/gather | solution.py:33
  389.3 10.8 %select_reduce_fusion.3 = f32[4096]{0:T(1024)S(1)} fusion(f32[4096,1440]{1,0:T(8,128)} %gather_fusion, s32[4096]{0:T(1024)S(1)} %bitcast.107), kind=kLoop, calls=%fused_computation.5.clone.1.clone | loop fusion | flops 17690624 | bytes 23625728 | tf_op jit(solution)/shard_map/while/body/eval_jaxpr/reduce_sum | solution.py:34
  400.1 0.2 dynamic_update_slice.7
  400.4 29.4 %gather_fusion = f32[4096,1440]{1,0:T(8,128)} fusion(f32[720,1440]{1,0:T(8,128)} %get-tuple-element.217, s32[4096]{0:T(1024)S(1)} %broadcast_clamp_fusion.3), kind=kCustom, calls=%fused_computation.clone.clone.1.clone | custom fusion | bytes 47202304 | tf_op jit(solution)/shard_map/while/body/eval_jaxpr/gather | solution.py:33
  429.8 10.8 %select_reduce_fusion.3 = f32[4096]{0:T(1024)S(1)} fusion(f32[4096,1440]{1,0:T(8,128)} %gather_fusion, s32[4096]{0:T(1024)S(1)} %bitcast.107), kind=kLoop, calls=%fused_computation.5.clone.1.clone | loop fusion | flops 17690624 | bytes 23625728 | tf_op jit(solution)/shard_map/while/body/eval_jaxpr/reduce_sum | solution.py:34
  440.6 0.2 dynamic_update_slice.7
  440.9 29.4 %gather_fusion = f32[4096,1440]{1,0:T(8,128)} fusion(f32[720,1440]{1,0:T(8,128)} %get-tuple-element.217, s32[4096]{0:T(1024)S(1)} %broadcast_clamp_fusion.3), kind=kCustom, calls=%fused_computation.clone.clone.1.clone | custom fusion | bytes 47202304 | tf_op jit(solution)/shard_map/while/body/eval_jaxpr/gather | solution.py:33
  470.4 10.8 %select_reduce_fusion.3 = f32[4096]{0:T(1024)S(1)} fusion(f32[4096,1440]{1,0:T(8,128)} %gather_fusion, s32[4096]{0:T(1024)S(1)} %bitcast.107), kind=kLoop, calls=%fused_computation.5.clone.1.clone | loop fusion | flops 17690624 | bytes 23625728 | tf_op jit(solution)/shard_map/while/body/eval_jaxpr/reduce_sum | solution.py:34
  481.2 0.2 dynamic_update_slice.7
  481.5 29.4 %gather_fusion = f32[4096,1440]{1,0:T(8,128)} fusion(f32[720,1440]{1,0:T(8,128)} %get-tuple-element.217, s32[4096]{0:T(1024)S(1)} %broadcast_clamp_fusion.3), kind=kCustom, calls=%fused_computation.clone.clone.1.clone | custom fusion | bytes 47202304 | tf_op jit(solution)/shard_map/while/body/eval_jaxpr/gather | solution.py:33
  511.0 10.8 %select_reduce_fusion.3 = f32[4096]{0:T(1024)S(1)} fusion(f32[4096,1440]{1,0:T(8,128)} %gather_fusion, s32[4096]{0:T(1024)S(1)} %bitcast.107), kind=kLoop, calls=%fused_computation.5.clone.1.clone | loop fusion | flops 17690624 | bytes 23625728 | tf_op jit(solution)/shard_map/while/body/eval_jaxpr/reduce_sum | solution.py:34
  521.7 0.2 dynamic_update_slice.7
  522.3 2.6 broadcast_in_dim.27
  524.9 188.8 %while.25 = (s32[]{:T(128)}, f32[720,1440]{1,0:T(8,128)}, s32[4,4096]{1,0:T(4,128)S(1)}, s32[4,4096]{1,0:T(4,128)S(1)}, f32[4,4096]{1,0:T(4,128)S(1)}) while((s32[]{:T(128)}, f32[720,1440]{1,0:T(8,128)}, s32[4,4096]{1,0:T(4,128)S(1)}, s32[4,4096]{1,0:T(4,128)S(1)}, f32[4,4096]{1,0:T(4,128)S(1)}) %tuple.52), condition=%wide.region_6.7_spmd.clone.clone, body=%wide.region_4.6_spmd.clone.sunk.clone | while | flops 17707008 | bytes 4278857 | solution.py:52
  525.0 47.1 %scatter_custom_fusion.8 = f32[720,1440]{1,0:T(8,128)} fusion(f32[720,1440]{1,0:T(8,128)} %get-tuple-element.224, s32[4096]{0:T(1024)S(1)} %bitcast.109, f32[]{:T(128)} %constant.35.clone.1..sunk.1, f32[4096]{0:T(1024)S(1)} %bitcast.105, s32[4096]{0:T(1024)S(1)} %bitcast.106), kind=kCustom, calls=%fused_computation.10.clone.1.clone | custom fusion | flops 17694720 | bytes 4180480 | tf_op jit(solution)/shard_map/while/body/eval_jaxpr/scatter-add | solution.py:48
  572.2 47.1 %scatter_custom_fusion.8 = f32[720,1440]{1,0:T(8,128)} fusion(f32[720,1440]{1,0:T(8,128)} %get-tuple-element.224, s32[4096]{0:T(1024)S(1)} %bitcast.109, f32[]{:T(128)} %constant.35.clone.1..sunk.1, f32[4096]{0:T(1024)S(1)} %bitcast.105, s32[4096]{0:T(1024)S(1)} %bitcast.106), kind=kCustom, calls=%fused_computation.10.clone.1.clone | custom fusion | flops 17694720 | bytes 4180480 | tf_op jit(solution)/shard_map/while/body/eval_jaxpr/scatter-add | solution.py:48
  619.4 47.1 %scatter_custom_fusion.8 = f32[720,1440]{1,0:T(8,128)} fusion(f32[720,1440]{1,0:T(8,128)} %get-tuple-element.224, s32[4096]{0:T(1024)S(1)} %bitcast.109, f32[]{:T(128)} %constant.35.clone.1..sunk.1, f32[4096]{0:T(1024)S(1)} %bitcast.105, s32[4096]{0:T(1024)S(1)} %bitcast.106), kind=kCustom, calls=%fused_computation.10.clone.1.clone | custom fusion | flops 17694720 | bytes 4180480 | tf_op jit(solution)/shard_map/while/body/eval_jaxpr/scatter-add | solution.py:48
  666.6 47.1 %scatter_custom_fusion.8 = f32[720,1440]{1,0:T(8,128)} fusion(f32[720,1440]{1,0:T(8,128)} %get-tuple-element.224, s32[4096]{0:T(1024)S(1)} %bitcast.109, f32[]{:T(128)} %constant.35.clone.1..sunk.1, f32[4096]{0:T(1024)S(1)} %bitcast.105, s32[4096]{0:T(1024)S(1)} %bitcast.106), kind=kCustom, calls=%fused_computation.10.clone.1.clone | custom fusion | flops 17694720 | bytes 4180480 | tf_op jit(solution)/shard_map/while/body/eval_jaxpr/scatter-add | solution.py:48
  713.7 4.2 broadcast_in_dim_reshape.3
  717.8 4.9 fusion.17
  722.7 2.7 copy.37
  725.4 8.9 all-to-all-start.2
  734.4 7.2 reshape.405
  741.6 12.2 %copy.38 = f32[1,1,720,1440]{2,3,0,1:T(8,128)} copy(f32[1,1,720,1440]{3,0,2,1:T(1,128)} %reshape.405) | data formatting | bytes 8294400 | tf_op jit(solution)/shard_map/convert_element_type | solution.py:98
  753.8 32.6 %all-to-all-done.2 = bf16[1,16,45,1440]{3,2,0,1:T(8,128)(2,1)} async-done(((bf16[1,16,45,1440]{3,2,0,1:T(8,128)(2,1)}), bf16[1,16,45,1440]{3,2,0,1:T(8,128)(2,1)}, u32[]{:S(2)}, u32[]{:S(2)}) %all-to-all-start.2) | async-done | bytes 2073632 | tf_op jit(solution)/shard_map/all_to_all | solution.py:96
  786.4 3.3 reshape.402
  789.8 11.8 %fusion.18 = bf16[1,1,720,1440]{2,3,0,1:T(8,128)(2,1)S(1)} fusion(f32[1,1,720,1440]{2,3,0,1:T(8,128)} %copy.38, bf16[720,1440]{1,0:T(8,128)(2,1)} %reshape.402, f32[]{:T(128)} %bitcast.1, f32[]{:T(128)} %bitcast, f32[1440]{0:T(1024)S(1)} %copy-done.12, f32[]{:T(128)} %bitcast.8, f32[]{:T(128)} %bitcast.7, f32[720]{0:T(1024)S(1)} %copy-done.14), kind=kOutput, calls=%fused_computation.31 | convolution fusion | flops 4506969600 | bytes 8303056 | tf_op jit(solution)/shard_map/lab,klbc->klac/dot_general | solution.py:22
  801.6 9.3 %copy.39 = bf16[1,1,720,1440]{3,0,1,2:T(2,128)(2,1)} copy(bf16[1,1,720,1440]{2,3,0,1:T(8,128)(2,1)S(1)} %fusion.18) | data formatting | bytes 4147200 | tf_op jit(solution)/shard_map/convert_element_type | solution.py:99
  810.9 14.0 %reduce.19 = bf16[720,1440]{1,0:T(8,128)(2,1)S(1)} reduce(bf16[720,1,1,1440]{3,2,1,0:T(2,128)(2,1)} %bitcast.102, bf16[]{:T(256)} %broadcast.349), dimensions={1,2}, to_apply=%bitcast.71.reduce_sub_computation | reduce | bytes 4147202
  824.9 5.1 reshape.464
  830.0 56.5 %all_to_all.40 = bf16[16,2,32400]{2,1,0:T(2,128)(2,1)S(1)} all-to-all(bf16[16,2,32400]{2,1,0:T(2,128)(2,1)} %reshape.464), channel_id=1, replica_groups=mesh['mem'=16,'tile'=16] {'tile'}, dimensions={0} | all-to-all | bytes 4147200 | tf_op jit(solution)/shard_map/all_to_all | solution.py:100
  886.5 8.7 reshape.465
  895.2 15.3 %bitcast_reduce_fusion = bf16[720,1440]{1,0:T(8,128)(2,1)} fusion(bf16[720,1,1,1440]{3,2,1,0:T(2,128)(2,1)} %reshape.465), kind=kLoop, calls=%fused_computation.51 | loop fusion | bytes 4147200 | tf_op jit(solution)/shard_map/all_to_all | solution.py:100
  910.4 2.0 all_to_all.14
  912.5 2.6 copy.40
  (64 shorter events, 0.7 us)
Async XLA Ops:
  6.5 13.8 %copy-start.15 = (f32[16]{0:T(128)S(1)}, f32[16]{0:T(128)}, u32[]{:S(2)}) copy-start(f32[16]{0:T(128)} %param.16) | copy-start | bytes 196
  6.5 15.2 %copy-start.16 = (f32[16]{0:T(128)S(1)}, f32[16]{0:T(128)}, u32[]{:S(2)}) copy-start(f32[16]{0:T(128)} %param.17) | copy-start | bytes 196
  10.8 62.5 %all-to-all-start = ((bf16[1,16,45,1440]{3,2,0,1:T(8,128)(2,1)}), bf16[1,16,45,1440]{3,2,0,1:T(8,128)(2,1)S(1)}, u32[]{:S(2)}, u32[]{:S(2)}) async-start(bf16[1,16,45,1440]{3,2,0,1:T(8,128)(2,1)} %copy.32), calls=%async_computation | async-start | bytes 4718592 | tf_op jit(solution)/shard_map/all_to_all | solution.py:84
  20.3 339.4 %all-reduce.2.cloned.1.call-start = ((), (), s32[]{:S(2)}) async-start(), calls=%async_computation.4 | async-start | bytes 8847360 | tf_op jit(solution)/shard_map/psum | solution.py:90
  23.2 64.2 %copy-start.13 = (f32[720]{0:T(1024)}, f32[720]{0:T(1024)S(1)}, u32[]{:S(2)}) copy-start(f32[720]{0:T(1024)S(1)} %iota_convert_fusion.1) | copy-start | bytes 8644
  23.2 64.1 %copy-start.11 = (f32[1440]{0:T(1024)}, f32[1440]{0:T(1024)S(1)}, u32[]{:S(2)}) copy-start(f32[1440]{0:T(1024)S(1)} %iota_convert_fusion) | copy-start | bytes 17284
  73.3 14.0 %copy-start = (bf16[1,16,45,1440]{3,2,0,1:T(8,128)(2,1)}, bf16[1,16,45,1440]{3,2,0,1:T(8,128)(2,1)S(1)}, u32[]{:S(2)}) copy-start(bf16[1,16,45,1440]{3,2,0,1:T(8,128)(2,1)S(1)} %all-to-all-done) | copy-start | bytes 6220804
  184.7 9.0 copy-start.2
  205.6 0.8 copy-start.8
  205.7 1.7 copy-start.6
  205.7 1.7 copy-start.7
  205.7 2.5 copy-start.9
  205.7 4.0 copy-start.10
  359.7 162.5 %copy-start.4 = (f32[4,4096]{1,0:T(4,128)S(1)}, f32[4,4096]{1,0:T(4,128)}, u32[]{:S(2)}) copy-start(f32[4,4096]{1,0:T(4,128)} %squeeze.23) | copy-start | bytes 196612
  359.7 162.5 %copy-start.5 = (f32[4,4096]{1,0:T(4,128)S(1)}, f32[4,4096]{1,0:T(4,128)}, u32[]{:S(2)}) copy-start(f32[4,4096]{1,0:T(4,128)} %squeeze.24) | copy-start | bytes 196612
  713.7 4.2 copy-start.3
  722.7 11.7 %copy-start.1 = (bf16[1,16,45,1440]{3,2,0,1:T(8,128)(2,1)S(1)}, bf16[1,16,45,1440]{3,2,0,1:T(8,128)(2,1)}, u32[]{:S(2)}) copy-start(bf16[1,16,45,1440]{3,2,0,1:T(8,128)(2,1)} %copy-done) | copy-start | bytes 6220804
  725.4 61.0 %all-to-all-start.2 = ((bf16[1,16,45,1440]{3,2,0,1:T(8,128)(2,1)}), bf16[1,16,45,1440]{3,2,0,1:T(8,128)(2,1)}, u32[]{:S(2)}, u32[]{:S(2)}) async-start(bf16[1,16,45,1440]{3,2,0,1:T(8,128)(2,1)} %copy.37), calls=%async_computation.2 | async-start | bytes 4718592 | tf_op jit(solution)/shard_map/all_to_all | solution.py:96
  753.8 35.9 %copy-start.12 = (f32[1440]{0:T(1024)S(1)}, f32[1440]{0:T(1024)}, u32[]{:S(2)}) copy-start(f32[1440]{0:T(1024)} %copy-done.11) | copy-start | bytes 17284
  753.8 35.9 %copy-start.14 = (f32[720]{0:T(1024)S(1)}, f32[720]{0:T(1024)}, u32[]{:S(2)}) copy-start(f32[720]{0:T(1024)} %copy-done.13) | copy-start | bytes 8644
Sparse Core Ops, SparseCore 0:
  205.8 153.8 all-reduce.1
where the time goes:
time: 932 us; the launch traced here: 922 us
  other arithmetic  279 us (30%)
  local copies, waits for them, and re-layouts  240 us (26%)
  waiting for transfers between devices  231 us (25%)
  blocking collectives  113 us (12%)
  matrix products  23.7 us (3%)
  starting transfers between devices  18.5 us (2%)
  between operations  15.9 us (2%)
    scatter-add x4, other arithmetic, place_one_block(): return (field.at[rows_here].add(lines, mode='drop'), jnp.float32(0.0))  188 us
    psum x1, waiting for transfers between devices, shards(): total_field = lax.psum(partial_field, 'mem')  148 us
    gather x4, local copies, waits for them, and re-layouts, pick_one_block(): taken = flat_rows[rows_here]  118 us
    all_to_all x1, blocking collectives, shards(): lax.all_to_all(spread_slab, 'tile', split_axis=2, concat_axis=1, tiled=True)  56.9 us
    all_to_all x1, blocking collectives, shards(): lax.all_to_all(gradient_slab, 'tile', split_axis=2, concat_axis=1, tiled=...  56.5 us
    all_to_all x1, waiting for transfers between devices, shards(): lax.all_to_all(alpha, 'tile', split_axis=1, concat_axis=2, tiled=True)  50.1 us
    reduce_sum x4, other arithmetic, pick_one_block(): jnp.sum(jnp.where(counter[None, :] == cols_here[:, None], taken, 0.0), ax...  43.1 us
    unnamed x42, local copies, waits for them, and re-layouts  34 us
  transfers between devices with their start and end apart: 3, of which 3 were waited for; matrix products, arithmetic and copies ran while one was open for 3% of the time, Pallas kernels for 0%

commit v1 on v0

--- a/solution.py
+++ b/solution.py
@@ -83,7 +83,9 @@
     band_line = level_index * row_count + row_index
     alpha_slab = lax.all_to_all(alpha, "tile", split_axis=1, concat_axis=2, tiled=True)
     spread_slab = localize(alpha_slab, lat_root, lon_root).astype(jnp.bfloat16)
-    spread_band = lax.all_to_all(spread_slab, "tile", split_axis=2, concat_axis=1, tiled=True)
+    shards_2 = jnp.split(spread_slab, lax.axis_size("tile"), axis=2)
+    received = lax.all_to_all(jnp.stack(shards_2), "tile", 0, 0)
+    spread_band = jnp.concatenate(received, axis=1)
     partial_field = jnp.sum(
         perturbation.astype(jnp.float32) * spread_band.astype(jnp.float32), axis=0
     )

time: 932 us -> 892 us (0.957)
  local copies, waits for them, and re-layouts: 240 us -> 215 us
  other arithmetic: 279 us -> 257 us
    convert_element_type x2 -> x0, local copies, waits for them, and re-layouts: 14.8 us -> none  [the longest x1 12.1 us: shards(): spread_slab = localize(alpha_slab, lat_root, lon_root).astype(jnp.bfloat16)]
    unnamed x5 -> x4, other arithmetic: 30.3 us -> 16.5 us
    unnamed x42 -> x57, local copies, waits for them, and re-layouts: 34 us -> 28 us
where the time goes in v1:
time: 892 us; the launch traced here: 882 us
  other arithmetic  257 us (29%)
  waiting for transfers between devices  231 us (26%)
  local copies, waits for them, and re-layouts  215 us (24%)
  blocking collectives  120 us (13%)
  matrix products  24.6 us (3%)
  starting transfers between devices  18.5 us (2%)
  between operations  15.9 us (2%)
    scatter-add x4, other arithmetic, place_one_block(): return (field.at[rows_here].add(lines, mode='drop'), jnp.float32(0.0))  188 us
    psum x1, waiting for transfers between devices, shards(): total_field = lax.psum(partial_field, 'mem')  148 us
    gather x4, local copies, waits for them, and re-layouts, pick_one_block(): taken = flat_rows[rows_here]  118 us
    all_to_all x1, blocking collectives, shards(): received = lax.all_to_all(jnp.stack(shards_2), 'tile', 0, 0)  63.5 us
    all_to_all x1, blocking collectives, shards(): lax.all_to_all(gradient_slab, 'tile', split_axis=2, concat_axis=1, tiled=...  56.5 us
    all_to_all x1, waiting for transfers between devices, shards(): lax.all_to_all(alpha, 'tile', split_axis=1, concat_axis=2, tiled=True)  50.3 us
    reduce_sum x4, other arithmetic, pick_one_block(): jnp.sum(jnp.where(counter[None, :] == cols_here[:, None], taken, 0.0), ax...  43.1 us
    all_to_all x1, waiting for transfers between devices, shards(): lax.all_to_all(sensitive, 'tile', split_axis=1, concat_axis=2, tiled=True)  32.7 us
  transfers between devices with their start and end apart: 3, of which 3 were waited for; matrix products, arithmetic and copies ran while one was open for 3% of the time, Pallas kernels for 0%

profile of v1, /device:TPU:34, one launch (start us, length us, event | category | flops | bytes accessed | tf_op | source)
XLA Modules:
  0.0 882.2 jit_solution(3734970085583548676)
XLA Ops:
  6.5 4.2 copy.50
  10.8 9.6 %all-to-all-start = ((bf16[1,16,45,1440]{3,2,0,1:T(8,128)(2,1)}), bf16[1,16,45,1440]{3,2,0,1:T(8,128)(2,1)S(1)}, u32[]{:S(2)}, u32[]{:S(2)}) async-start(bf16[1,16,45,1440]{3,2,0,1:T(8,128)(2,1)} %copy.50), calls=%async_computation | async-start | bytes 4718592 | tf_op jit(solution)/shard_map/all_to_all | solution.py:84
  20.5 0.6 dynamic_slice.23
  21.8 0.6 dynamic_slice.24
  23.1 50.3 %all-to-all-done = bf16[1,16,45,1440]{3,2,0,1:T(8,128)(2,1)S(1)} async-done(((bf16[1,16,45,1440]{3,2,0,1:T(8,128)(2,1)}), bf16[1,16,45,1440]{3,2,0,1:T(8,128)(2,1)S(1)}, u32[]{:S(2)}, u32[]{:S(2)}) %all-to-all-start) | async-done | bytes 2073632 | tf_op jit(solution)/shard_map/all_to_all | solution.py:84
  73.4 2.1 reshape.397
  75.6 12.9 %convolution_convert_fusion = bf16[1440,720]{0,1:T(8,128)(2,1)} fusion(bf16[720,1440]{1,0:T(8,128)(2,1)} %reshape.397, f32[]{:T(128)} %bitcast.1, f32[]{:T(128)} %bitcast, f32[1440]{0:T(1024)S(1)} %iota_convert_fusion, f32[]{:T(128)} %bitcast.8, f32[]{:T(128)} %bitcast.7, f32[720]{0:T(1024)S(1)} %iota_convert_fusion.1), kind=kOutput, calls=%fused_computation.36 | convolution fusion | flops 4505932800 | bytes 4155856 | tf_op jit(solution)/shard_map/lab,klbc->klac/dot_general | solution.py:22
  88.5 1.1 fusion.58
  89.6 1.0 fusion.57
  90.6 1.0 fusion.56
  91.5 1.0 fusion.55
  92.5 1.0 fusion.54
  93.4 1.0 fusion.53
  94.4 1.0 fusion.52
  95.4 1.0 fusion.51
  96.7 63.5 %all_to_all.35 = bf16[16,1,1,45,1440]{4,3,2,1,0:T(8,128)(2,1)S(1)} all-to-all(bf16[16,1,1,45,1440]{4,3,2,1,0:T(8,128)(2,1)S(1)} %fusion.43), channel_id=1, replica_groups=mesh['mem'=16,'tile'=16] {'tile'}, dimensions={0} | all-to-all | bytes 4147200 | tf_op jit(solution)/shard_map/all_to_all | solution.py:87
  160.2 3.7 convert_multiply_fusion.1
  163.8 4.1 reshape.399
  168.0 0.5 broadcast.346
  168.5 0.3 copy-done.9
  168.7 0.8 reduce.14
  169.6 0.2 add_reduce_fusion
  169.8 0.6 broadcast.347
  170.4 0.8 reduce.15
  171.3 0.7 squeeze.23
  171.9 0.8 reduce.16
  172.8 0.6 squeeze.24
  174.1 147.9 %all-reduce.2.cloned.1.call-done = f32[720,1440]{1,0:T(8,128)} async-done(((f32[720,1440]{1,0:T(8,128)}), f32[720,1440]{1,0:T(8,128)}) %all-reduce.2.cloned.1.call-update) | async-done | bytes 4147216 | tf_op jit(solution)/shard_map/psum | solution.py:92
  322.0 162.3 %while.24 = (s32[]{:T(128)}, f32[4,4096]{1,0:T(4,128)S(1)}, s32[4,4096]{1,0:T(4,128)S(1)}, s32[4,4096]{1,0:T(4,128)S(1)}, f32[720,1440]{1,0:T(8,128)}) while((s32[]{:T(128)}, f32[4,4096]{1,0:T(4,128)S(1)}, s32[4,4096]{1,0:T(4,128)S(1)}, s32[4,4096]{1,0:T(4,128)S(1)}, f32[720,1440]{1,0:T(8,128)}) %tuple.43), condition=%wide.region_3.4_spmd.clone.clone, body=%wide.region_1.3_spmd.clone.sunk.clone | while | flops 17707008 | bytes 70959168 | solution.py:36
  322.1 29.5 %gather_fusion = f32[4096,1440]{1,0:T(8,128)} fusion(f32[720,1440]{1,0:T(8,128)} %get-tuple-element.217, s32[4096]{0:T(1024)S(1)} %broadcast_clamp_fusion.3), kind=kCustom, calls=%fused_computation.clone.clone.1.clone | custom fusion | bytes 47202304 | tf_op jit(solution)/shard_map/while/body/eval_jaxpr/gather | solution.py:33
  351.6 10.8 %select_reduce_fusion.3 = f32[4096]{0:T(1024)S(1)} fusion(f32[4096,1440]{1,0:T(8,128)} %gather_fusion, s32[4096]{0:T(1024)S(1)} %bitcast.201), kind=kLoop, calls=%fused_computation.5.clone.1.clone | loop fusion | flops 17690624 | bytes 23625728 | tf_op jit(solution)/shard_map/while/body/eval_jaxpr/reduce_sum | solution.py:34
  362.3 0.2 dynamic_update_slice.7
  362.6 29.5 %gather_fusion = f32[4096,1440]{1,0:T(8,128)} fusion(f32[720,1440]{1,0:T(8,128)} %get-tuple-element.217, s32[4096]{0:T(1024)S(1)} %broadcast_clamp_fusion.3), kind=kCustom, calls=%fused_computation.clone.clone.1.clone | custom fusion | bytes 47202304 | tf_op jit(solution)/shard_map/while/body/eval_jaxpr/gather | solution.py:33
  392.1 10.8 %select_reduce_fusion.3 = f32[4096]{0:T(1024)S(1)} fusion(f32[4096,1440]{1,0:T(8,128)} %gather_fusion, s32[4096]{0:T(1024)S(1)} %bitcast.201), kind=kLoop, calls=%fused_computation.5.clone.1.clone | loop fusion | flops 17690624 | bytes 23625728 | tf_op jit(solution)/shard_map/while/body/eval_jaxpr/reduce_sum | solution.py:34
  402.9 0.2 dynamic_update_slice.7
  403.2 29.5 %gather_fusion = f32[4096,1440]{1,0:T(8,128)} fusion(f32[720,1440]{1,0:T(8,128)} %get-tuple-element.217, s32[4096]{0:T(1024)S(1)} %broadcast_clamp_fusion.3), kind=kCustom, calls=%fused_computation.clone.clone.1.clone | custom fusion | bytes 47202304 | tf_op jit(solution)/shard_map/while/body/eval_jaxpr/gather | solution.py:33
  432.7 10.8 %select_reduce_fusion.3 = f32[4096]{0:T(1024)S(1)} fusion(f32[4096,1440]{1,0:T(8,128)} %gather_fusion, s32[4096]{0:T(1024)S(1)} %bitcast.201), kind=kLoop, calls=%fused_computation.5.clone.1.clone | loop fusion | flops 17690624 | bytes 23625728 | tf_op jit(solution)/shard_map/while/body/eval_jaxpr/reduce_sum | solution.py:34
  443.5 0.2 dynamic_update_slice.7
  443.8 29.5 %gather_fusion = f32[4096,1440]{1,0:T(8,128)} fusion(f32[720,1440]{1,0:T(8,128)} %get-tuple-element.217, s32[4096]{0:T(1024)S(1)} %broadcast_clamp_fusion.3), kind=kCustom, calls=%fused_computation.clone.clone.1.clone | custom fusion | bytes 47202304 | tf_op jit(solution)/shard_map/while/body/eval_jaxpr/gather | solution.py:33
  473.3 10.8 %select_reduce_fusion.3 = f32[4096]{0:T(1024)S(1)} fusion(f32[4096,1440]{1,0:T(8,128)} %gather_fusion, s32[4096]{0:T(1024)S(1)} %bitcast.201), kind=kLoop, calls=%fused_computation.5.clone.1.clone | loop fusion | flops 17690624 | bytes 23625728 | tf_op jit(solution)/shard_map/while/body/eval_jaxpr/reduce_sum | solution.py:34
  484.0 0.2 dynamic_update_slice.7
  484.4 2.6 broadcast_in_dim.27
  487.0 188.7 %while.25 = (s32[]{:T(128)}, f32[720,1440]{1,0:T(8,128)}, s32[4,4096]{1,0:T(4,128)S(1)}, s32[4,4096]{1,0:T(4,128)S(1)}, f32[4,4096]{1,0:T(4,128)S(1)}) while((s32[]{:T(128)}, f32[720,1440]{1,0:T(8,128)}, s32[4,4096]{1,0:T(4,128)S(1)}, s32[4,4096]{1,0:T(4,128)S(1)}, f32[4,4096]{1,0:T(4,128)S(1)}) %tuple.52), condition=%wide.region_6.7_spmd.clone.clone, body=%wide.region_4.6_spmd.clone.sunk.clone | while | flops 17707008 | bytes 4278857 | solution.py:52
  487.1 47.1 %scatter_custom_fusion.8 = f32[720,1440]{1,0:T(8,128)} fusion(f32[720,1440]{1,0:T(8,128)} %get-tuple-element.224, s32[4096]{0:T(1024)S(1)} %bitcast.203, f32[]{:T(128)} %constant.35.clone.1..sunk.1, f32[4096]{0:T(1024)S(1)} %bitcast.199, s32[4096]{0:T(1024)S(1)} %bitcast.200), kind=kCustom, calls=%fused_computation.10.clone.1.clone | custom fusion | flops 17694720 | bytes 4180480 | tf_op jit(solution)/shard_map/while/body/eval_jaxpr/scatter-add | solution.py:48
  534.3 47.1 %scatter_custom_fusion.8 = f32[720,1440]{1,0:T(8,128)} fusion(f32[720,1440]{1,0:T(8,128)} %get-tuple-element.224, s32[4096]{0:T(1024)S(1)} %bitcast.203, f32[]{:T(128)} %constant.35.clone.1..sunk.1, f32[4096]{0:T(1024)S(1)} %bitcast.199, s32[4096]{0:T(1024)S(1)} %bitcast.200), kind=kCustom, calls=%fused_computation.10.clone.1.clone | custom fusion | flops 17694720 | bytes 4180480 | tf_op jit(solution)/shard_map/while/body/eval_jaxpr/scatter-add | solution.py:48
  581.4 47.1 %scatter_custom_fusion.8 = f32[720,1440]{1,0:T(8,128)} fusion(f32[720,1440]{1,0:T(8,128)} %get-tuple-element.224, s32[4096]{0:T(1024)S(1)} %bitcast.203, f32[]{:T(128)} %constant.35.clone.1..sunk.1, f32[4096]{0:T(1024)S(1)} %bitcast.199, s32[4096]{0:T(1024)S(1)} %bitcast.200), kind=kCustom, calls=%fused_computation.10.clone.1.clone | custom fusion | flops 17694720 | bytes 4180480 | tf_op jit(solution)/shard_map/while/body/eval_jaxpr/scatter-add | solution.py:48
  628.6 47.1 %scatter_custom_fusion.8 = f32[720,1440]{1,0:T(8,128)} fusion(f32[720,1440]{1,0:T(8,128)} %get-tuple-element.224, s32[4096]{0:T(1024)S(1)} %bitcast.203, f32[]{:T(128)} %constant.35.clone.1..sunk.1, f32[4096]{0:T(1024)S(1)} %bitcast.199, s32[4096]{0:T(1024)S(1)} %bitcast.200), kind=kCustom, calls=%fused_computation.10.clone.1.clone | custom fusion | flops 17694720 | bytes 4180480 | tf_op jit(solution)/shard_map/while/body/eval_jaxpr/scatter-add | solution.py:48
  675.7 4.2 broadcast_in_dim_reshape.3
  679.9 5.2 fusion.35
  685.1 8.8 %all-to-all-start.2 = ((bf16[1,16,45,1440]{3,2,0,1:T(8,128)(2,1)}), bf16[1,16,45,1440]{3,2,0,1:T(8,128)(2,1)}, u32[]{:S(2)}, u32[]{:S(2)}) async-start(bf16[1,16,45,1440]{3,2,0,1:T(8,128)(2,1)} %fusion.35), calls=%async_computation.2 | async-start | bytes 4718592 | tf_op jit(solution)/shard_map/all_to_all | solution.py:98
  694.0 7.3 reshape.403
  701.2 12.1 %copy.68 = f32[1,1,720,1440]{2,3,0,1:T(8,128)} copy(f32[1,1,720,1440]{3,0,2,1:T(1,128)} %reshape.403) | data formatting | bytes 8294400 | tf_op jit(solution)/shard_map/convert_element_type | solution.py:100
  713.4 32.7 %all-to-all-done.2 = bf16[1,16,45,1440]{3,2,0,1:T(8,128)(2,1)} async-done(((bf16[1,16,45,1440]{3,2,0,1:T(8,128)(2,1)}), bf16[1,16,45,1440]{3,2,0,1:T(8,128)(2,1)}, u32[]{:S(2)}, u32[]{:S(2)}) %all-to-all-start.2) | async-done | bytes 2073632 | tf_op jit(solution)/shard_map/all_to_all | solution.py:98
  746.0 3.3 reshape.400
  749.4 11.7 %fusion.18 = bf16[1,1,720,1440]{2,3,0,1:T(8,128)(2,1)S(1)} fusion(f32[1,1,720,1440]{2,3,0,1:T(8,128)} %copy.68, bf16[720,1440]{1,0:T(8,128)(2,1)} %reshape.400, f32[]{:T(128)} %bitcast.1, f32[]{:T(128)} %bitcast, f32[1440]{0:T(1024)S(1)} %copy-done.13, f32[]{:T(128)} %bitcast.8, f32[]{:T(128)} %bitcast.7, f32[720]{0:T(1024)S(1)} %copy-done.15), kind=kOutput, calls=%fused_computation.31 | convolution fusion | flops 4506969600 | bytes 8303056 | tf_op jit(solution)/shard_map/lab,klbc->klac/dot_general | solution.py:22
  761.1 9.3 %copy.69 = bf16[1,1,720,1440]{3,0,1,2:T(2,128)(2,1)} copy(bf16[1,1,720,1440]{2,3,0,1:T(8,128)(2,1)S(1)} %fusion.18) | data formatting | bytes 4147200 | tf_op jit(solution)/shard_map/convert_element_type | solution.py:101
  770.4 0.5 broadcast.349
  770.9 14.1 %reduce.18 = bf16[720,1440]{1,0:T(8,128)(2,1)S(1)} reduce(bf16[720,1,1,1440]{3,2,1,0:T(2,128)(2,1)} %bitcast.181, bf16[]{:T(256)} %broadcast.349), dimensions={1,2}, to_apply=%bitcast.151.reduce_sub_computation | reduce | bytes 4147202
  784.9 5.1 reshape.460
  790.0 56.5 %all_to_all.36 = bf16[16,2,32400]{2,1,0:T(2,128)(2,1)S(1)} all-to-all(bf16[16,2,32400]{2,1,0:T(2,128)(2,1)} %reshape.460), channel_id=1, replica_groups=mesh['mem'=16,'tile'=16] {'tile'}, dimensions={0} | all-to-all | bytes 4147200 | tf_op jit(solution)/shard_map/all_to_all | solution.py:102
  846.5 8.7 reshape.461
  855.2 15.3 %bitcast_reduce_fusion = bf16[720,1440]{1,0:T(8,128)(2,1)} fusion(bf16[720,1,1,1440]{3,2,1,0:T(2,128)(2,1)} %reshape.461), kind=kLoop, calls=%fused_computation.83 | loop fusion | bytes 4147200 | tf_op jit(solution)/shard_map/all_to_all | solution.py:102
  870.5 2.0 all_to_all.14
  872.5 2.6 copy.70
  (75 shorter events, 1.0 us)
Async XLA Ops:
  10.8 9.7 %copy-start.16 = (f32[16]{0:T(128)S(1)}, f32[16]{0:T(128)}, u32[]{:S(2)}) copy-start(f32[16]{0:T(128)} %param.16) | copy-start | bytes 196
  10.8 11.0 %copy-start.17 = (f32[16]{0:T(128)S(1)}, f32[16]{0:T(128)}, u32[]{:S(2)}) copy-start(f32[16]{0:T(128)} %param.17) | copy-start | bytes 196
  10.8 62.6 %all-to-all-start = ((bf16[1,16,45,1440]{3,2,0,1:T(8,128)(2,1)}), bf16[1,16,45,1440]{3,2,0,1:T(8,128)(2,1)S(1)}, u32[]{:S(2)}, u32[]{:S(2)}) async-start(bf16[1,16,45,1440]{3,2,0,1:T(8,128)(2,1)} %copy.50), calls=%async_computation | async-start | bytes 4718592 | tf_op jit(solution)/shard_map/all_to_all | solution.py:84
  20.4 301.6 %all-reduce.2.cloned.1.call-start = ((), (), s32[]{:S(2)}) async-start(), calls=%async_computation.4 | async-start | bytes 8847360 | tf_op jit(solution)/shard_map/psum | solution.py:92
  23.1 65.4 %copy-start.14 = (f32[720]{0:T(1024)}, f32[720]{0:T(1024)S(1)}, u32[]{:S(2)}) copy-start(f32[720]{0:T(1024)S(1)} %iota_convert_fusion.1) | copy-start | bytes 8644
  23.1 65.4 %copy-start.12 = (f32[1440]{0:T(1024)}, f32[1440]{0:T(1024)S(1)}, u32[]{:S(2)}) copy-start(f32[1440]{0:T(1024)S(1)} %iota_convert_fusion) | copy-start | bytes 17284
  73.4 15.1 %copy-start = (bf16[1,16,45,1440]{3,2,0,1:T(8,128)(2,1)}, bf16[1,16,45,1440]{3,2,0,1:T(8,128)(2,1)S(1)}, u32[]{:S(2)}) copy-start(bf16[1,16,45,1440]{3,2,0,1:T(8,128)(2,1)S(1)} %all-to-all-done) | copy-start | bytes 6220804
  88.5 7.8 copy-start.4
  96.7 63.5 %copy-start.2 = (bf16[1,16,45,1440]{3,1,2,0:T(8,128)(2,1)S(1)}, bf16[1,16,45,1440]{3,1,2,0:T(8,128)(2,1)}, u32[]{:S(2)}) copy-start(bf16[1,16,45,1440]{3,1,2,0:T(8,128)(2,1)} %param.15) | copy-start | bytes 6220804
  167.9 0.8 copy-start.9
  167.9 1.7 copy-start.7
  167.9 1.7 copy-start.8
  167.9 2.5 copy-start.10
  167.9 4.0 copy-start.11
  322.0 162.3 %copy-start.5 = (f32[4,4096]{1,0:T(4,128)S(1)}, f32[4,4096]{1,0:T(4,128)}, u32[]{:S(2)}) copy-start(f32[4,4096]{1,0:T(4,128)} %squeeze.23) | copy-start | bytes 196612
  322.0 162.3 %copy-start.6 = (f32[4,4096]{1,0:T(4,128)S(1)}, f32[4,4096]{1,0:T(4,128)}, u32[]{:S(2)}) copy-start(f32[4,4096]{1,0:T(4,128)} %squeeze.24) | copy-start | bytes 196612
  675.7 4.2 copy-start.3
  685.1 8.9 %copy-start.1 = (bf16[1,16,45,1440]{3,2,0,1:T(8,128)(2,1)S(1)}, bf16[1,16,45,1440]{3,2,0,1:T(8,128)(2,1)}, u32[]{:S(2)}) copy-start(bf16[1,16,45,1440]{3,2,0,1:T(8,128)(2,1)} %copy-done) | copy-start | bytes 6220804
  685.1 60.9 %all-to-all-start.2 = ((bf16[1,16,45,1440]{3,2,0,1:T(8,128)(2,1)}), bf16[1,16,45,1440]{3,2,0,1:T(8,128)(2,1)}, u32[]{:S(2)}, u32[]{:S(2)}) async-start(bf16[1,16,45,1440]{3,2,0,1:T(8,128)(2,1)} %fusion.35), calls=%async_computation.2 | async-start | bytes 4718592 | tf_op jit(solution)/shard_map/all_to_all | solution.py:98
  713.4 36.0 %copy-start.13 = (f32[1440]{0:T(1024)S(1)}, f32[1440]{0:T(1024)}, u32[]{:S(2)}) copy-start(f32[1440]{0:T(1024)} %copy-done.12) | copy-start | bytes 17284
  713.4 36.0 %copy-start.15 = (f32[720]{0:T(1024)S(1)}, f32[720]{0:T(1024)}, u32[]{:S(2)}) copy-start(f32[720]{0:T(1024)} %copy-done.14) | copy-start | bytes 8644
Sparse Core Ops, SparseCore 0:
  168.1 153.8 all-reduce.1
